TPU v7x, 32 devices: a whole 2x2x4 slice. The times are simulated.
32 devices in a mesh: clip: 2 (over x), tm: 4 (over z), chan: 4 (over y, core).
Axes of the slice: x: 2, y: 2, z: 4, core: 2. Of those that a mesh axis runs over, the one named last changes fastest.
Arguments:
- signal: bfloat16 [2, 4096, 256], P('clip', 'tm', 'chan'), may hold values from -6 to 6
- conv_first: bfloat16 [3, 256, 128], P(None, 'chan'), may hold values from -0.21875 to 0.21875
- conv_second: bfloat16 [128, 256], P(None, 'chan'), may hold values from -0.5 to 0.5
- conv_down: bfloat16 [16, 256, 512], P(None, 'chan'), may hold values from -0.09375 to 0.09375
- cotangent: bfloat16 [2, 512, 512], P('clip', 'tm'), may hold values from -6 to 6
Outputs:
- grad_signal: bfloat16 [2, 4096, 256], P('clip', 'tm', 'chan')
- grad_first: float32 [3, 256, 128], P(None, 'chan')
- grad_second: float32 [128, 256], P(None, 'chan')
- grad_down: float32 [16, 256, 512], P(None, 'chan')
All inputs are finite; a program needn't handle non-finite values.
Results may differ from a plain program's by a relative error of at most 0.018.
Values may be sent and summed in bfloat16 or wider, within the bound.
No kernel may reach another device: no remote copies, remote signals or barrier semaphores. Data moves between devices by JAX's collectives and lax.ppermute only.
A program may use at most 64 MiB of HBM per device.

v0:
```python
import jax
import jax.numpy as jnp
from jax import lax
from jax.sharding import PartitionSpec as P

KRES = 3
STRIDE = 8
RIM = 10


def shifted(block, axis, distance):
    devices = range(lax.axis_size(axis))
    route = [(i - distance, i) for i in devices if i - distance in devices]
    return lax.ppermute(block, axis, route)


def elu(value):
    return jnp.where(value > 0, value, jnp.exp(jnp.minimum(value, 0.0)) - 1.0)


def slope(value):
    return jnp.where(value > 0, 1.0, jnp.exp(jnp.minimum(value, 0.0)))


def contract_rows(left, right):
    return lax.dot_general(
        left, right, (((0,), (0,)), ((), ())), preferred_element_type=jnp.float32
    )


def contract_cols(left, right):
    return lax.dot_general(
        left, right, (((1,), (1,)), ((), ())), preferred_element_type=jnp.float32
    )


def causal_conv(values, weights, span):
    total = jnp.zeros((span, weights.shape[2]), jnp.float32)
    for k in range(KRES):
        total = total + jnp.dot(
            values[k : k + span], weights[k], preferred_element_type=jnp.float32
        )
    return total


def on_device(signal, conv_first, conv_second, conv_down, cotangent):
    frames = signal[0]
    length, local_ch = frames.shape
    span = length + RIM - KRES + 1
    borrowed = shifted(frames[length - RIM :], "tm", 1)
    padded = jnp.concatenate([borrowed, frames], axis=0)
    act = elu(padded.astype(jnp.float32)).astype(jnp.bfloat16)
    hidden = lax.psum(causal_conv(act, conv_first, span).astype(jnp.bfloat16), "chan").astype(
        jnp.float32
    )
    inner = elu(hidden).astype(jnp.bfloat16)
    resid = padded[KRES - 1 :].astype(jnp.float32) + jnp.dot(
        inner, conv_second, preferred_element_type=jnp.float32
    )
    feed = elu(resid).astype(jnp.bfloat16)
    blocks = feed.reshape(span // STRIDE, STRIDE * local_ch)
    wide = conv_down.reshape(2, STRIDE * local_ch, conv_down.shape[2])
    upstream = cotangent[0]
    count = upstream.shape[0]
    front = contract_cols(upstream, wide[0])
    back = contract_cols(upstream, wide[1])
    dblocks = jnp.pad(front, ((0, 1), (0, 0))) + jnp.pad(back, ((1, 0), (0, 0)))
    down_raw = jnp.stack(
        [contract_rows(blocks[:count], upstream), contract_rows(blocks[1:], upstream)]
    )
    down_raw = down_raw.reshape(conv_down.shape)
    dresid = dblocks.reshape(span, local_ch) * slope(resid)
    dres16 = dresid.astype(jnp.bfloat16)
    second_raw = contract_rows(inner, dres16)
    dinner = lax.psum(contract_cols(dres16, conv_second).astype(jnp.bfloat16), "chan").astype(
        jnp.float32
    )
    dhid = (dinner * slope(hidden)).astype(jnp.bfloat16)
    first_raw = jnp.stack([contract_rows(act[k : k + span], dhid) for k in range(KRES)])
    dact = jnp.zeros(padded.shape, jnp.float32)
    for k in range(KRES):
        dact = dact + jnp.pad(contract_cols(dhid, conv_first[k]), ((k, KRES - 1 - k), (0, 0)))
    dpadded = dact * slope(padded.astype(jnp.float32)) + jnp.pad(dresid, ((KRES - 1, 0), (0, 0)))
    returned = shifted(dpadded[:RIM], "tm", -1)
    grad_frames = dpadded[RIM:] + jnp.pad(returned, ((length - RIM, 0), (0, 0)))
    first_total, second_total, down_total = lax.psum(
        (first_raw, second_raw, down_raw), ("clip", "tm")
    )
    factor = 1.0 / jnp.sqrt(
        jnp.float32(lax.axis_size("clip") * lax.axis_size("tm") * (length // STRIDE))
    )
    return (
        grad_frames.astype(jnp.bfloat16)[None],
        first_total * factor,
        second_total * factor,
        down_total * factor,
    )


def solution(mesh):
    return jax.shard_map(
        on_device,
        mesh=mesh,
        in_specs=(
            P("clip", "tm", "chan"),
            P(None, "chan", None),
            P(None, "chan"),
            P(None, "chan", None),
            P("clip", "tm", None),
        ),
        out_specs=(
            P("clip", "tm", "chan"),
            P(None, "chan", None),
            P(None, "chan"),
            P(None, "chan", None),
        ),
        check_vma=False,
    )
```

profile of v0, /device:TPU:0, one launch (start us, length us, event | category | flops | bytes accessed | tf_op | source)
XLA Modules:
  0.0 208.7 jit_solution(13187131113075802272)
XLA Ops:
  7.2 0.9 slice_bitcast_fusion
  8.1 4.9 %collective-permute-start = (bf16[10,64]{0,1:T(8,128)(2,1)S(1)}, bf16[10,64]{0,1:T(8,128)(2,1)S(1)}, u32[]{:S(2)}, u32[]{:S(2)}) collective-permute-start(bf16[10,64]{0,1:T(8,128)(2,1)S(1)} %slice_bitcast_fusion), channel_id=1, source_target_pairs={{0,4},{4,8},{8,12},{1,5},{5,9},{9,13},{2,6},{6,10},{10,14},{3,7},{... | collective-permute-start | bytes 3848 | tf_op jit(solution)/shard_map/ppermute | solution.py:14
  13.0 1.3 fusion.56
  14.8 0.3 fusion.29
  15.2 0.5 convolution_add_fusion.1
  15.6 1.2 fusion
  17.6 32.4 %all-reduce.12.cloned.1.call-done = bf16[1032,128]{1,0:T(8,128)(2,1)} async-done(((bf16[1032,128]{1,0:T(8,128)(2,1)}), bf16[1032,128]{1,0:T(8,128)(2,1)}) %all-reduce.12.cloned.1.call-update) | async-done | bytes 264208 | tf_op jit(solution)/shard_map/psum | solution.py:53
  50.0 1.3 fusion.9
  52.2 1.0 convolution_convert_fusion
  53.3 0.3 convolution_bitcast_fusion
  53.6 0.3 convolution_bitcast_fusion.1
  54.0 1.5 pad_maximum_fusion
  55.4 30.2 %all-reduce.14.cloned.1.call-done = bf16[1032,128]{1,0:T(8,128)(2,1)} async-done(((bf16[1032,128]{1,0:T(8,128)(2,1)}), bf16[1032,128]{1,0:T(8,128)(2,1)}) %all-reduce.14.cloned.1.call-update) | async-done | bytes 264208 | tf_op jit(solution)/shard_map/psum | solution.py:75
  85.6 1.1 fusion.3
  87.4 0.7 pad_maximum_fusion.2
  88.4 39.2 %psum.38 = f32[128,64]{0,1:T(8,128)S(1)} all-reduce(f32[128,64]{0,1:T(8,128)S(1)} %fusion.31), channel_id=1, replica_groups=mesh['clip'=2,'tm'=4,'chan'=4] {'clip','tm'}, use_global_device_ids=true, to_apply=%region_3.4 | all-reduce | flops 8192 | bytes 65536 | tf_op jit(solution)/shard_map/psum | solution.py:86
  128.2 0.3 fusion.11
  128.6 1.3 collective-permute-start.1
  129.9 0.6 broadcast_multiply_fusion.2
  130.5 3.9 %collective-permute-done.1 = f32[10,64]{0,1:T(8,128)S(1)} collective-permute-done((f32[10,64]{0,1:T(8,128)S(1)}, f32[10,64]{0,1:T(8,128)S(1)}, u32[]{:S(2)}, u32[]{:S(2)}) %collective-permute-start.1) | collective-permute-done | bytes 2592 | tf_op jit(solution)/shard_map/ppermute | solution.py:14
  134.4 0.8 fusion.17
  135.2 62.3 %all-reduce.16.cloned.1.call-done = (f32[3,64,128]{2,1,0:T(8,128)}, f32[16,64,512]{2,1,0:T(8,128)}) async-done(((f32[3,64,128]{2,1,0:T(8,128)}, f32[16,64,512]{2,1,0:T(8,128)}), (f32[3,64,128]{2,1,0:T(8,128)}, f32[16,64,512]{2,1,0:T(8,128)})) %all-reduce.16.cloned.1.call-update) | async-done | bytes 2195472 | tf_op jit(solution)/shard_map/psum | solution.py:86
  197.5 1.5 broadcast_multiply_fusion.1
  199.0 3.2 %broadcast_multiply_fusion = f32[16,64,512]{2,1,0:T(8,128)} fusion(f32[16,64,512]{2,1,0:T(8,128)} %get-tuple-element.5), kind=kLoop, calls=%fused_computation.10 | loop fusion | flops 524288 | bytes 4194304 | tf_op jit(solution)/shard_map/mul | solution.py:96
  (36 shorter events, 3.8 us)
Async XLA Ops:
  7.2 7.2 %copy-start = (bf16[1,128,512]{2,1,0:T(8,128)(2,1)S(1)}, bf16[1,128,512]{2,1,0:T(8,128)(2,1)}, u32[]{:S(2)}) copy-start(bf16[1,128,512]{2,1,0:T(8,128)(2,1)} %param.9) | copy-start | bytes 393220
  7.2 7.5 %copy-start.1 = (bf16[1,1024,64]{1,2,0:T(8,128)(2,1)S(1)}, bf16[1,1024,64]{1,2,0:T(8,128)(2,1)}, u32[]{:S(2)}) copy-start(bf16[1,1024,64]{1,2,0:T(8,128)(2,1)} %param.5) | copy-start | bytes 393220
  7.2 7.6 %copy-start.3 = (bf16[3,64,128]{2,1,0:T(8,128)(2,1)S(1)}, bf16[3,64,128]{2,1,0:T(8,128)(2,1)}, u32[]{:S(2)}) copy-start(bf16[3,64,128]{2,1,0:T(8,128)(2,1)} %param.6) | copy-start | bytes 147460
  7.2 42.8 %all-reduce.12.cloned.1.call-start = ((), (), s32[]{:S(2)}) async-start(), calls=%async_computation | async-start | bytes 528384 | tf_op jit(solution)/shard_map/psum | solution.py:53
  8.1 6.5 %collective-permute-start = (bf16[10,64]{0,1:T(8,128)(2,1)S(1)}, bf16[10,64]{0,1:T(8,128)(2,1)S(1)}, u32[]{:S(2)}, u32[]{:S(2)}) collective-permute-start(bf16[10,64]{0,1:T(8,128)(2,1)S(1)} %slice_bitcast_fusion), channel_id=1, source_target_pairs={{0,4},{4,8},{8,12},{1,5},{5,9},{9,13},{2,6},{6,10},{10,14},{3,7},{... | collective-permute-start | bytes 3848 | tf_op jit(solution)/shard_map/ppermute | solution.py:14
  15.6 34.4 %copy-start.4 = (bf16[128,64]{0,1:T(8,128)(2,1)S(1)}, bf16[128,64]{0,1:T(8,128)(2,1)}, u32[]{:S(2)}) copy-start(bf16[128,64]{0,1:T(8,128)(2,1)} %param.7) | copy-start | bytes 49156
  16.8 68.8 %all-reduce.14.cloned.1.call-start = ((), (), s32[]{:S(2)}) async-start(), calls=%async_computation.1 | async-start | bytes 528384 | tf_op jit(solution)/shard_map/psum | solution.py:75
  53.3 144.2 %all-reduce.16.cloned.1.call-start = ((), (), s32[]{:S(2)}) async-start(), calls=%async_computation.2 | async-start | bytes 4390912 | tf_op jit(solution)/shard_map/psum | solution.py:86
  53.9 31.7 %copy-start.2 = (bf16[1032,128]{1,0:T(8,128)(2,1)S(1)}, bf16[1032,128]{1,0:T(8,128)(2,1)}, u32[]{:S(2)}) copy-start(bf16[1032,128]{1,0:T(8,128)(2,1)} %all-reduce.12.cloned.1.call-done) | copy-start | bytes 792580
  128.6 5.8 %collective-permute-start.1 = (f32[10,64]{0,1:T(8,128)S(1)}, f32[10,64]{0,1:T(8,128)S(1)}, u32[]{:S(2)}, u32[]{:S(2)}) collective-permute-start(f32[10,64]{0,1:T(8,128)S(1)} %slice.82), channel_id=1, source_target_pairs={{4,0},{8,4},{12,8},{5,1},{9,5},{13,9},{6,2},{10,6},{14,10},{7,3},{... | collective-permute-start | bytes 7688 | tf_op jit(solution)/shard_map/ppermute | solution.py:14
Sparse Core Ops, SparseCore 0:
  16.9 32.9 all-reduce.11
  53.4 32.2 all-reduce.13
  90.0 107.4 all-reduce.15
where the time goes:
time: 209 us
  waiting for transfers between devices  129 us (62%)
  blocking collectives  39.2 us (19%)
  between operations  13.9 us (7%)
  other arithmetic  9.89 us (5%)
  matrix products  7.15 us (3%)
  starting transfers between devices  6.33 us (3%)
  local copies, waits for them, and re-layouts  3.4 us (2%)
    psum x1, waiting for transfers between devices, on_device(): lax.psum((first_raw, second_raw, down_raw), ('clip', 'tm'))  62.3 us
    psum x1, blocking collectives, on_device(): lax.psum((first_raw, second_raw, down_raw), ('clip', 'tm'))  39.2 us
    psum x1, waiting for transfers between devices, on_device(): lax.psum(causal_conv(act, conv_first, span).astype(jnp.bfloat16), 'chan')  32.4 us
    psum x1, waiting for transfers between devices, on_device(): lax.psum(contract_cols(dres16, conv_second).astype(jnp.bfloat16), 'chan')  30.2 us
    ppermute x2, starting transfers between devices, shifted(): return lax.ppermute(block, axis, route)  6.21 us
  transfers between devices with their start and end apart: 5, of which 4 were waited for; matrix products, arithmetic and copies ran while one was open for 3% of the time, Pallas kernels for 0%

commit v1 on v0

--- a/solution.py
+++ b/solution.py
@@ -84,7 +84,7 @@
     returned = shifted(dpadded[:RIM], "tm", -1)
     grad_frames = dpadded[RIM:] + jnp.pad(returned, ((length - RIM, 0), (0, 0)))
     first_total, second_total, down_total = lax.psum(
-        (first_raw, second_raw, down_raw), ("clip", "tm")
+        lax.psum((first_raw, second_raw, down_raw), "tm"), "clip"
     )
     factor = 1.0 / jnp.sqrt(
         jnp.float32(lax.axis_size("clip") * lax.axis_size("tm") * (length // STRIDE))

time: 209 us -> 259 us (1.24)
  waiting for transfers between devices: 129 us -> 192 us
  blocking collectives: 39.2 us -> 26 us
    psum x1 -> x2, waiting for transfers between devices: 62.3 us -> 125 us  [the longest x1 92.1 us: on_device(): lax.psum((first_raw, second_raw, down_raw), 'tm')]
    psum x1 -> x2, blocking collectives: 39.2 us -> 26 us  [the longest x1 16.8 us: on_device(): lax.psum((first_raw, second_raw, down_raw), 'tm')]
  transfers between devices with their start and end apart: 5 -> 6, of which waited for: 4 -> 5; matrix products, arithmetic and copies ran while one was open for 3% -> 3% of each run, Pallas kernels for 0% -> 0%
where the time goes in v1:
time: 259 us
  waiting for transfers between devices  192 us (74%)
  blocking collectives  26 us (10%)
  between operations  14 us (5%)
  other arithmetic  9.89 us (4%)
  matrix products  7.14 us (3%)
  starting transfers between devices  6.37 us (2%)
  local copies, waits for them, and re-layouts  3.39 us (1%)
    psum x1, waiting for transfers between devices, on_device(): lax.psum((first_raw, second_raw, down_raw), 'tm')  92.1 us
    psum x1, waiting for transfers between devices, on_device(): lax.psum(lax.psum((first_raw, second_raw, down_raw), 'tm'), 'clip')  33.3 us
    psum x1, waiting for transfers between devices, on_device(): lax.psum(causal_conv(act, conv_first, span).astype(jnp.bfloat16), 'chan')  32.4 us
    psum x1, waiting for transfers between devices, on_device(): lax.psum(contract_cols(dres16, conv_second).astype(jnp.bfloat16), 'chan')  30.2 us
    psum x1, blocking collectives, on_device(): lax.psum((first_raw, second_raw, down_raw), 'tm')  16.8 us
    psum x1, blocking collectives, on_device(): lax.psum(lax.psum((first_raw, second_raw, down_raw), 'tm'), 'clip')  9.19 us
    ppermute x2, starting transfers between devices, shifted(): return lax.ppermute(block, axis, route)  6.21 us
  transfers between devices with their start and end apart: 6, of which 5 were waited for; matrix products, arithmetic and copies ran while one was open for 3% of the time, Pallas kernels for 0%

profile of v1, /device:TPU:0, one launch (start us, length us, event | category | flops | bytes accessed | tf_op | source)
XLA Modules:
  0.0 258.8 jit_solution(11523423065642519106)
XLA Ops:
  7.2 0.9 slice_bitcast_fusion
  8.1 4.9 %collective-permute-start = (bf16[10,64]{0,1:T(8,128)(2,1)S(1)}, bf16[10,64]{0,1:T(8,128)(2,1)S(1)}, u32[]{:S(2)}, u32[]{:S(2)}) collective-permute-start(bf16[10,64]{0,1:T(8,128)(2,1)S(1)} %slice_bitcast_fusion), channel_id=1, source_target_pairs={{0,4},{4,8},{8,12},{1,5},{5,9},{9,13},{2,6},{6,10},{10,14},{3,7},{... | collective-permute-start | bytes 3848 | tf_op jit(solution)/shard_map/ppermute | solution.py:14
  13.0 1.3 fusion.56
  14.8 0.3 fusion.29
  15.2 0.5 convolution_add_fusion.1
  15.6 1.2 fusion
  17.6 32.4 %all-reduce.14.cloned.1.call-done = bf16[1032,128]{1,0:T(8,128)(2,1)} async-done(((bf16[1032,128]{1,0:T(8,128)(2,1)}), bf16[1032,128]{1,0:T(8,128)(2,1)}) %all-reduce.14.cloned.1.call-update) | async-done | bytes 264208 | tf_op jit(solution)/shard_map/psum | solution.py:53
  50.0 1.3 fusion.9
  52.2 1.0 convolution_convert_fusion
  53.9 1.5 pad_maximum_fusion
  55.4 30.2 %all-reduce.16.cloned.1.call-done = bf16[1032,128]{1,0:T(8,128)(2,1)} async-done(((bf16[1032,128]{1,0:T(8,128)(2,1)}), bf16[1032,128]{1,0:T(8,128)(2,1)}) %all-reduce.16.cloned.1.call-update) | async-done | bytes 264208 | tf_op jit(solution)/shard_map/psum | solution.py:75
  85.6 1.1 fusion.3
  87.4 0.7 pad_maximum_fusion.2
  88.1 92.1 %all-reduce.18.cloned.1.call-done = (f32[3,64,128]{2,1,0:T(8,128)}, f32[16,64,512]{2,1,0:T(8,128)}) async-done(((f32[3,64,128]{2,1,0:T(8,128)}, f32[16,64,512]{2,1,0:T(8,128)}), (f32[3,64,128]{2,1,0:T(8,128)}, f32[16,64,512]{2,1,0:T(8,128)})) %all-reduce.18.cloned.1.call-update) | async-done | bytes 2195472 | tf_op jit(solution)/shard_map/psum | solution.py:87
  180.6 16.8 %psum.60 = f32[128,64]{0,1:T(8,128)S(1)} all-reduce(f32[128,64]{0,1:T(8,128)S(1)} %fusion.31), channel_id=1, replica_groups=mesh['clip'=2,'tm'=4,'chan'=4] {'tm'}, use_global_device_ids=true, to_apply=%region_4.5 | all-reduce | flops 8192 | bytes 65536 | tf_op jit(solution)/shard_map/psum | solution.py:87
  197.4 9.2 %psum.61 = f32[128,64]{0,1:T(8,128)S(1)} all-reduce(f32[128,64]{0,1:T(8,128)S(1)} %psum.60), channel_id=1, replica_groups=mesh['clip'=2,'tm'=4,'chan'=4] {'clip'}, use_global_device_ids=true, to_apply=%region_5.6 | all-reduce | flops 8192 | bytes 65536 | tf_op jit(solution)/shard_map/psum | solution.py:86
  207.3 0.3 fusion.11
  207.6 1.3 collective-permute-start.1
  208.9 0.6 broadcast_multiply_fusion.2
  209.5 3.9 %collective-permute-done.1 = f32[10,64]{0,1:T(8,128)S(1)} collective-permute-done((f32[10,64]{0,1:T(8,128)S(1)}, f32[10,64]{0,1:T(8,128)S(1)}, u32[]{:S(2)}, u32[]{:S(2)}) %collective-permute-start.1) | collective-permute-done | bytes 2592 | tf_op jit(solution)/shard_map/ppermute | solution.py:14
  213.4 0.8 fusion.17
  214.2 33.3 %all-reduce.20.cloned.1.call-done = (f32[3,64,128]{2,1,0:T(8,128)}, f32[16,64,512]{2,1,0:T(8,128)}) async-done(((f32[3,64,128]{2,1,0:T(8,128)}, f32[16,64,512]{2,1,0:T(8,128)}), (f32[3,64,128]{2,1,0:T(8,128)}, f32[16,64,512]{2,1,0:T(8,128)})) %all-reduce.20.cloned.1.call-update) | async-done | bytes 2195472 | tf_op jit(solution)/shard_map/psum | solution.py:86
  247.5 1.5 broadcast_multiply_fusion.1
  249.1 3.2 %broadcast_multiply_fusion = f32[16,64,512]{2,1,0:T(8,128)} fusion(f32[16,64,512]{2,1,0:T(8,128)} %get-tuple-element.7), kind=kLoop, calls=%fused_computation.10 | loop fusion | flops 524288 | bytes 4194304 | tf_op jit(solution)/shard_map/mul | solution.py:96
  (40 shorter events, 4.5 us)
Async XLA Ops:
  7.2 7.2 %copy-start = (bf16[1,128,512]{2,1,0:T(8,128)(2,1)S(1)}, bf16[1,128,512]{2,1,0:T(8,128)(2,1)}, u32[]{:S(2)}) copy-start(bf16[1,128,512]{2,1,0:T(8,128)(2,1)} %param.9) | copy-start | bytes 393220
  7.2 7.5 %copy-start.1 = (bf16[1,1024,64]{1,2,0:T(8,128)(2,1)S(1)}, bf16[1,1024,64]{1,2,0:T(8,128)(2,1)}, u32[]{:S(2)}) copy-start(bf16[1,1024,64]{1,2,0:T(8,128)(2,1)} %param.5) | copy-start | bytes 393220
  7.2 7.6 %copy-start.3 = (bf16[3,64,128]{2,1,0:T(8,128)(2,1)S(1)}, bf16[3,64,128]{2,1,0:T(8,128)(2,1)}, u32[]{:S(2)}) copy-start(bf16[3,64,128]{2,1,0:T(8,128)(2,1)} %param.6) | copy-start | bytes 147460
  7.2 42.8 %all-reduce.14.cloned.1.call-start = ((), (), s32[]{:S(2)}) async-start(), calls=%async_computation | async-start | bytes 528384 | tf_op jit(solution)/shard_map/psum | solution.py:53
  8.1 6.5 %collective-permute-start = (bf16[10,64]{0,1:T(8,128)(2,1)S(1)}, bf16[10,64]{0,1:T(8,128)(2,1)S(1)}, u32[]{:S(2)}, u32[]{:S(2)}) collective-permute-start(bf16[10,64]{0,1:T(8,128)(2,1)S(1)} %slice_bitcast_fusion), channel_id=1, source_target_pairs={{0,4},{4,8},{8,12},{1,5},{5,9},{9,13},{2,6},{6,10},{10,14},{3,7},{... | collective-permute-start | bytes 3848 | tf_op jit(solution)/shard_map/ppermute | solution.py:14
  15.6 34.4 %copy-start.4 = (bf16[128,64]{0,1:T(8,128)(2,1)S(1)}, bf16[128,64]{0,1:T(8,128)(2,1)}, u32[]{:S(2)}) copy-start(bf16[128,64]{0,1:T(8,128)(2,1)} %param.7) | copy-start | bytes 49156
  16.8 68.8 %all-reduce.16.cloned.1.call-start = ((), (), s32[]{:S(2)}) async-start(), calls=%async_computation.1 | async-start | bytes 528384 | tf_op jit(solution)/shard_map/psum | solution.py:75
  53.2 127.0 %all-reduce.18.cloned.1.call-start = ((), (), s32[]{:S(2)}) async-start(), calls=%async_computation.2 | async-start | bytes 4390912 | tf_op jit(solution)/shard_map/psum | solution.py:87
  53.9 31.7 %copy-start.2 = (bf16[1032,128]{1,0:T(8,128)(2,1)S(1)}, bf16[1032,128]{1,0:T(8,128)(2,1)}, u32[]{:S(2)}) copy-start(bf16[1032,128]{1,0:T(8,128)(2,1)} %all-reduce.14.cloned.1.call-done) | copy-start | bytes 792580
  88.1 159.4 %all-reduce.20.cloned.1.call-start = ((), (), s32[]{:S(2)}) async-start(), calls=%async_computation.3 | async-start | bytes 4390912 | tf_op jit(solution)/shard_map/psum | solution.py:86
  207.6 5.8 %collective-permute-start.1 = (f32[10,64]{0,1:T(8,128)S(1)}, f32[10,64]{0,1:T(8,128)S(1)}, u32[]{:S(2)}, u32[]{:S(2)}) collective-permute-start(f32[10,64]{0,1:T(8,128)S(1)} %slice.82), channel_id=1, source_target_pairs={{4,0},{8,4},{12,8},{5,1},{9,5},{13,9},{6,2},{10,6},{14,10},{7,3},{... | collective-permute-start | bytes 7688 | tf_op jit(solution)/shard_map/ppermute | solution.py:14
Sparse Core Ops, SparseCore 0:
  16.9 32.9 all-reduce.13
  53.4 32.2 all-reduce.15
  88.6 91.5 all-reduce.17
  182.5 64.9 all-reduce.19
